TPU v7x, 32 devices: a whole 2x2x4 slice. The times are simulated.
32 devices in a mesh: groups: 2 (over y), seq: 4 (over z), head: 2 (over x), dp: 2 (over core).
Axes of the slice: x: 2, y: 2, z: 4, core: 2. Of those that a mesh axis runs over, the one named last changes fastest.
Arguments:
- queries: bfloat16 [4, 2048, 512], P(('groups', 'dp'), 'seq', 'head'), parts along dimension 0, may hold values from -6 to 6
- key_rows: bfloat16 [4, 2048, 512], P(('groups', 'dp'), 'seq', 'head'), parts along dimension 0, may hold values from -6 to 6
- value_rows: bfloat16 [4, 2048, 512], P(('groups', 'dp'), 'seq', 'head'), parts along dimension 0, may hold values from -6 to 6
- layout: int32 [4, 8, 4], P('head'), may hold values from 0 to 7
- out_weight: bfloat16 [4096, 512], P(None, 'head'), may hold values from -0.25 to 0.25
- out_grad: bfloat16 [4, 2048, 4096], P(('groups', 'dp'), 'seq', 'head'), parts along dimension 0, may hold values from -6 to 6
Outputs:
- attn: bfloat16 [4, 2048, 512], P(('groups', 'dp'), 'seq', 'head'), parts along dimension 0
- query_grad: bfloat16 [4, 2048, 512], P(('groups', 'dp'), 'seq', 'head'), parts along dimension 0
- key_grad: bfloat16 [4, 2048, 512], P(('groups', 'dp'), 'seq', 'head'), parts along dimension 0
- value_grad: bfloat16 [4, 2048, 512], P(('groups', 'dp'), 'seq', 'head'), parts along dimension 0
- weight_grad: float32 [8192, 512], P(('groups', 'seq', 'dp'), 'head'), parts along dimension 0
There are 2 independent parts, one for each index of `groups`. A program takes and returns all parts, laid end to end along the dimension named above; an argument that names none is the same for every part. Nothing has to cross between parts.
Inputs may be any that keep to these rules, and one draw needn't show every extreme that they name: layout[h, i, j] names a key-value block of the same sequence that query block i of head h reads; entries may repeat and may name any block.
All inputs are finite; a program needn't handle non-finite values.
Results may differ from a plain program's by a relative error of at most 0.018.
Values may be sent and summed in bfloat16 or wider, within the bound.
No kernel may reach another device: no remote copies, remote signals or barrier semaphores. Data moves between devices by JAX's collectives and lax.ppermute only.
A program may use at most 64 MiB of HBM per device.

v0:
```python
import jax
import jax.numpy as jnp
from jax import lax
from jax.sharding import PartitionSpec as P

DH = 128
BLK = 256
epsilon = 1e-06


def feature_map(inputs):
    return jnp.where(inputs > 0, inputs + 1.0, jnp.exp(jnp.minimum(inputs, 0.0)))


def feature_slope(inputs):
    return jnp.where(inputs > 0, 1.0, jnp.exp(jnp.minimum(inputs, 0.0)))


def per_device(queries, key_rows, value_rows, layout, out_weight, out_grad):
    highest = lax.Precision.HIGHEST
    f32 = jnp.float32
    bf16 = jnp.bfloat16
    seq_count = lax.axis_size("seq")
    seq_index = lax.axis_index("seq")
    heads_here = layout.shape[0]
    block_total = layout.shape[1]
    tokens_here = queries.shape[1]
    block_count = tokens_here // BLK
    my_first = seq_index * block_count
    counts = jnp.sum(
        (layout[..., None] == jnp.arange(block_total, dtype=jnp.int32)).astype(f32), axis=2
    )
    owner_cols = lax.dynamic_slice_in_dim(counts, my_first, block_count, 2)
    causal = jnp.tril(jnp.ones((BLK, BLK), f32))
    query_in = queries[0].astype(f32).reshape(block_count, BLK, heads_here, DH)
    key_in = key_rows[0].astype(f32).reshape(block_count, BLK, heads_here, DH)
    value_b = value_rows[0].reshape(block_count, BLK, heads_here, DH)
    query_feat = feature_map(query_in).astype(bf16)
    key_feat = feature_map(key_in).astype(bf16)
    states = jnp.einsum("nthd,nthe->nhde", key_feat, value_b, preferred_element_type=f32)
    presum = jnp.einsum("hqm,mhde->qhde", owner_cols, states, precision=highest)
    presum = presum.reshape(seq_count, block_count, heads_here, DH, DH)
    arrived = lax.all_to_all(presum, "seq", split_axis=0, concat_axis=0, tiled=True)
    carried = jnp.sum(arrived, axis=0)
    carried_b = carried.astype(bf16)
    scores = (
        jnp.einsum("nthd,nshd->nhts", query_feat, key_feat, preferred_element_type=f32) * causal
    )
    scores_b = scores.astype(bf16)
    numer = jnp.einsum("nthd,nhde->nthe", query_feat, carried_b, preferred_element_type=f32)
    numer = numer + jnp.einsum("nhts,nshe->nthe", scores_b, value_b, preferred_element_type=f32)
    rinv = lax.rsqrt(jnp.mean(numer * numer, axis=-1, keepdims=True) + epsilon)
    attn_out = (numer * rinv).astype(bf16)
    attn_flat = attn_out.reshape(tokens_here, heads_here * DH)
    gathered = lax.all_gather(out_grad, "head", axis=2, tiled=True)
    grad_rows = gathered[0]
    d_attn = jnp.dot(grad_rows, out_weight, preferred_element_type=f32).astype(bf16)
    grad_f = d_attn.astype(f32).reshape(block_count, BLK, heads_here, DH)
    d_numer = rinv * grad_f - numer * rinv**3 * jnp.mean(grad_f * numer, axis=-1, keepdims=True)
    d_numer = d_numer.astype(bf16)
    c_grad = jnp.einsum("nthd,nthe->nhde", query_feat, d_numer, preferred_element_type=f32)
    s_grad = jnp.einsum(
        "hmk,mhde->khde",
        owner_cols,
        lax.all_gather(c_grad, "seq", axis=0, tiled=True),
        precision=highest,
    )
    s_grad_b = s_grad.astype(bf16)
    p_grad = (
        jnp.einsum("nthe,nshe->nhts", d_numer, value_b, preferred_element_type=f32) * causal
    ).astype(bf16)
    dq_feat = jnp.einsum("nthe,nhde->nthd", d_numer, carried_b, preferred_element_type=f32)
    dq_feat = dq_feat + jnp.einsum("nhts,nshd->nthd", p_grad, key_feat, preferred_element_type=f32)
    dk_feat = jnp.einsum("nshe,nhde->nshd", value_b, s_grad_b, preferred_element_type=f32)
    dk_feat = dk_feat + jnp.einsum(
        "nhts,nthd->nshd", p_grad, query_feat, preferred_element_type=f32
    )
    dv_full = jnp.einsum("nshd,nhde->nshe", key_feat, s_grad_b, preferred_element_type=f32)
    dv_full = dv_full + jnp.einsum("nhts,nthe->nshe", scores_b, d_numer, preferred_element_type=f32)
    flat_shape = (1, tokens_here, heads_here * DH)
    query_grad = (dq_feat * feature_slope(query_in)).astype(bf16).reshape(flat_shape)
    key_grad = (dk_feat * feature_slope(key_in)).astype(bf16).reshape(flat_shape)
    value_grad = dv_full.astype(bf16).reshape(flat_shape)
    weight_grad = lax.psum_scatter(
        lax.dot_general(
            grad_rows, attn_flat, (((0,), (0,)), ((), ())), preferred_element_type=f32
        ).astype(jnp.bfloat16),
        ("seq", "dp"),
        scatter_dimension=0,
        tiled=True,
    ).astype(jnp.float32)
    return (attn_flat.reshape(flat_shape), query_grad, key_grad, value_grad, weight_grad)


def solution(mesh):
    placed = (
        P(("groups", "dp"), "seq", "head"),
        P(("groups", "dp"), "seq", "head"),
        P(("groups", "dp"), "seq", "head"),
        P("head", None, None),
        P(None, "head"),
        P(("groups", "dp"), "seq", "head"),
    )
    return jax.shard_map(
        per_device,
        mesh=mesh,
        in_specs=placed,
        out_specs=(
            P(("groups", "dp"), "seq", "head"),
            P(("groups", "dp"), "seq", "head"),
            P(("groups", "dp"), "seq", "head"),
            P(("groups", "dp"), "seq", "head"),
            P(("groups", "seq", "dp"), "head"),
        ),
        check_vma=False,
    )
```

profile of v0, /device:TPU:0, one launch (start us, length us, event | category | flops | bytes accessed | tf_op | source)
XLA Modules:
  0.0 156.0 jit_solution(2445478102337339927)
XLA Ops:
  7.2 0.7 all-gather.3.cloned.1.call-update
  7.9 1.9 %fusion.26 = (f32[1,512,256]{2,1,0:T(8,128)}, bf16[1,512,256]{2,1,0:T(8,128)(2,1)S(1)}) fusion(bf16[1,512,256]{2,1,0:T(8,128)(2,1)} %param.7), kind=kLoop, calls=%fused_computation.37 | loop fusion | flops 917504 | bytes 1048576 | tf_op jit(solution)/shard_map/jit(_where)/select_n | solution.py:16
  9.9 0.1 copy.86
  10.2 0.1 convert_reduce_fusion
  10.2 0.2 fusion.41
  10.5 1.1 fusion.33
  11.6 1.4 copy.90
  13.0 6.3 %all-to-all-start = ((f32[4,2,2,128,128]{4,1,3,2,0:T(2,128)}), f32[4,2,2,128,128]{4,1,3,2,0:T(2,128)}, u32[]{:S(2)}, u32[]{:S(2)}) async-start(f32[4,2,2,128,128]{4,1,3,2,0:T(2,128)} %copy.90), calls=%async_computation | async-start | bytes 2097152 | tf_op jit(solution)/shard_map/all_to_all | solution.py:43
  19.3 2.0 %fusion.30 = (f32[1,512,256]{2,1,0:T(8,128)}, bf16[1,512,256]{2,1,0:T(8,128)(2,1)S(1)}) fusion(bf16[1,512,256]{2,1,0:T(8,128)(2,1)} %param.6), kind=kLoop, calls=%fused_computation.41 | loop fusion | flops 917504 | bytes 1048576 | tf_op jit(solution)/shard_map/jit(_where)/select_n | solution.py:16
  21.3 0.1 copy.107
  21.5 0.3 fusion.4
  21.9 0.4 copy-done.4
  22.2 1.1 convolution_bitcast_fusion
  23.4 21.7 %all-to-all-done = f32[4,2,2,128,128]{4,1,3,2,0:T(2,128)} async-done(((f32[4,2,2,128,128]{4,1,3,2,0:T(2,128)}), f32[4,2,2,128,128]{4,1,3,2,0:T(2,128)}, u32[]{:S(2)}, u32[]{:S(2)}) %all-to-all-start) | async-done | bytes 1048608 | tf_op jit(solution)/shard_map/all_to_all | solution.py:43
  45.1 1.7 %reduce_sum.37 = bf16[2,2,128,128]{3,0,2,1:T(2,128)(2,1)S(1)} reduce(f32[4,2,2,128,128]{4,1,3,2,0:T(2,128)} %all-to-all-done, f32[]{:T(128)} %constant.9.clone.1), dimensions={0}, to_apply=%region_1.2 | reduce | flops 196608 | bytes 1179652 | tf_op jit(solution)/shard_map/reduce_sum | solution.py:44
  46.8 22.2 %all-gather.3.cloned.1.call-done = bf16[1,512,4096]{2,1,0:T(8,128)(2,1)} async-done(((bf16[1,512,2048]{2,1,0:T(8,128)(2,1)}), bf16[1,512,4096]{2,1,0:T(8,128)(2,1)}) %all-gather.3.cloned.1.call-update) | async-done | bytes 4194320 | tf_op jit(solution)/shard_map/all_gather | solution.py:55
  69.1 4.2 %fusion.16 = f32[512,256]{1,0:T(8,128)} fusion(bf16[4096,256]{1,0:T(8,128)(2,1)S(1)} %copy-done, bf16[1,512,4096]{2,1,0:T(8,128)(2,1)} %all-gather.3.cloned.1.call-done), kind=kOutput, calls=%fused_computation.22 | convolution fusion | flops 1074003968 | bytes 6815744 | tf_op jit(solution)/shard_map/dot_general | solution.py:57
  73.3 2.1 %reshape.94 = f32[2,256,2,128]{3,2,1,0:T(2,128)} reshape(f32[512,256]{1,0:T(8,128)} %fusion.16) | data formatting | bytes 1048576 | tf_op jit(solution)/shard_map/reshape | solution.py:58
  75.4 2.0 %copy.98 = f32[2,256,2,128]{1,3,2,0:T(8,128)} copy(f32[2,256,2,128]{3,2,1,0:T(2,128)} %reshape.94) | data formatting | bytes 1048576 | tf_op jit(solution)/shard_map/reshape | solution.py:58
  77.4 1.5 multiply_reduce_fusion
  79.0 1.9 %subtract_convert_fusion = (bf16[2,256,2,128]{1,3,2,0:T(8,128)(2,1)S(1)}, bf16[2,256,2,128]{1,3,2,0:T(8,128)(2,1)}) fusion(f32[2,256,2,128]{1,3,2,0:T(8,128)S(1)} %get-tuple-element.35, f32[2,256,2,128]{1,3,2,0:T(8,128)} %copy.98, f32[2,256,2]{1,2,0:T(2,128)S(1)} %get-tuple-element.36, f32[2,256,2]{1,2,0:T(2,128)S(1)} %get-tuple-element.33, ...), kind=kLoop, calls=%fused_computation.42 | loop fusion | flops 917504 | bytes 1585152 | tf_op jit(solution)/shard_map/convert_element_type | solution.py:60
  80.8 1.0 fusion.52
  81.8 0.2 reduce-scatter.2.cloned.1.call-start
  82.1 1.8 %copy.97 = bf16[2,256,2,128]{3,2,1,0:T(2,128)(2,1)} copy(bf16[2,256,2,128]{1,3,2,0:T(8,128)(2,1)} %get-tuple-element.28) | data formatting | bytes 524288 | tf_op jit(solution)/shard_map/convert_element_type | solution.py:53
  83.9 4.9 %fusion = bf16[4096,256]{0,1:T(8,128)(2,1)} fusion(bf16[1,512,4096]{2,1,0:T(8,128)(2,1)} %all-gather.3.cloned.1.call-done, bf16[64,8,2,128]{3,2,1,0:T(2,128)(2,1)} %bitcast.68), kind=kOutput, calls=%fused_computation.1 | convolution fusion | flops 1074790400 | bytes 6553600 | tf_op jit(solution)/shard_map/dot_general | solution.py:85
  88.8 2.1 %select_n.48 = f32[2,256,2,128]{3,2,1,0:T(2,128)} reshape(f32[1,512,256]{2,1,0:T(8,128)} %get-tuple-element.29) | data formatting | bytes 1048576 | tf_op jit(solution)/shard_map/jit(_where)/select_n | solution.py:16
  90.9 2.0 %copy.113 = f32[2,256,2,128]{1,3,2,0:T(8,128)} copy(f32[2,256,2,128]{3,2,1,0:T(2,128)} %select_n.48) | data formatting | bytes 1048576 | tf_op jit(solution)/shard_map/jit(_where)/select_n | solution.py:16
  92.9 2.1 %select_n.46 = f32[2,256,2,128]{3,2,1,0:T(2,128)} reshape(f32[1,512,256]{2,1,0:T(8,128)} %get-tuple-element.31) | data formatting | bytes 1048576 | tf_op jit(solution)/shard_map/jit(_where)/select_n | solution.py:16
  95.0 2.0 %copy.105 = f32[2,256,2,128]{1,3,2,0:T(8,128)} copy(f32[2,256,2,128]{3,2,1,0:T(2,128)} %select_n.46) | data formatting | bytes 1048576 | tf_op jit(solution)/shard_map/jit(_where)/select_n | solution.py:16
  97.1 1.8 %reshape_reshape.3 = bf16[1,512,256]{2,1,0:T(8,128)(2,1)} reshape(bf16[2,256,2,128]{3,2,1,0:T(2,128)(2,1)} %copy.97) | data formatting | bytes 524288 | tf_op jit(solution)/shard_map/reshape;reshape | solution.py:92
  98.9 1.3 fusion.5
  100.2 0.8 copy-done.1
  101.0 1.3 fusion.51
  102.2 2.0 %fusion.11 = bf16[2,256,2,128]{1,3,2,0:T(8,128)(2,1)} fusion(f32[2,256,2,128]{1,3,2,0:T(8,128)} %copy.105, f32[2,2,128,256]{3,2,1,0:T(8,128)S(1)} %fusion.51, bf16[2,256,2,128]{1,3,2,0:T(8,128)(2,1)S(1)} %get-tuple-element.27, bf16[2,2,128,128]{3,0,2,1:T(2,128)(2,1)S(1)} %reduce_sum.37), kind=kOutput, calls=%fused_computation.19 | convolution fusion | flops 33947648 | bytes 1703936 | tf_op jit(solution)/shard_map/nthe,nhde->nthd/dot_general | solution.py:72
  104.2 1.8 %copy.106 = bf16[2,256,2,128]{3,2,1,0:T(2,128)(2,1)} copy(bf16[2,256,2,128]{1,3,2,0:T(8,128)(2,1)} %fusion.11) | data formatting | bytes 524288 | tf_op jit(solution)/shard_map/convert_element_type | solution.py:81
  106.0 1.8 %reshape.89 = bf16[1,512,256]{2,1,0:T(8,128)(2,1)} reshape(bf16[2,256,2,128]{3,2,1,0:T(2,128)(2,1)} %copy.106) | data formatting | bytes 524288 | tf_op jit(solution)/shard_map/reshape | solution.py:81
  107.9 1.0 fusion.54
  108.9 2.1 %fusion.53 = f32[2,2,128,256]{3,2,1,0:T(8,128)} fusion(bf16[2,256,2,128]{1,3,2,0:T(8,128)(2,1)S(1)} %copy.107, bf16[2,2,256,256]{3,2,1,0:T(8,128)(2,1)} %copy-done.1), kind=kOutput, calls=%fused_computation.74 | convolution fusion | flops 67108864 | bytes 1310720 | tf_op jit(solution)/shard_map/nhts,nthd->nshd/dot_general | solution.py:75
  111.0 2.9 %fusion.21 = bf16[2,2,128,128]{3,0,2,1:T(2,128)(2,1)S(1)} fusion(f32[8,2,128,128]{3,2,1,0:T(8,128)} %all-gather.5.cloned.1.call-done, f32[2,8,8]{2,1,0:T(8,128)S(1)} %convert_reduce_fusion, s32[]{:T(128)S(6)} %select_n.41), kind=kOutput, calls=%fused_computation.26 | convolution fusion | flops 6356992 | bytes 1180164 | tf_op jit(solution)/shard_map/hmk,mhde->khde/dot_general | solution.py:62
  113.9 0.1 copy.115
  114.0 2.1 %fusion.20 = bf16[2,256,2,128]{1,3,2,0:T(8,128)(2,1)} fusion(f32[2,2,128,256]{3,2,1,0:T(8,128)} %fusion.54, bf16[2,2,128,128]{2,3,1,0:T(8,128)(2,1)S(1)} %copy.115, bf16[2,256,2,128]{3,2,1,0:T(2,128)(2,1)} %copy-done.2), kind=kOutput, calls=%fused_computation.24 | convolution fusion | flops 33816576 | bytes 1179648 | tf_op jit(solution)/shard_map/nshd,nhde->nshe/dot_general | solution.py:78
  116.1 1.1 copy.117
  117.2 0.9 reshape.91
  118.1 1.3 fusion.12
  119.4 0.2 copy.114
  119.6 0.9 reshape.90
  120.4 27.1 %reduce-scatter.2.cloned.1.call-done = bf16[512,256]{0,1:T(8,128)(2,1)} async-done(((bf16[4096,256]{0,1:T(8,128)(2,1)}), bf16[512,256]{0,1:T(8,128)(2,1)}) %reduce-scatter.2.cloned.1.call-update) | async-done | bytes 262160 | tf_op jit(solution)/shard_map/reduce_scatter | solution.py:84
  147.6 1.9 %copy.119 = f32[512,256]{1,0:T(8,128)} copy(bf16[512,256]{0,1:T(8,128)(2,1)} %reduce-scatter.2.cloned.1.call-done) | data formatting | bytes 786432
  (24 shorter events, 0.3 us)
Async XLA Ops:
  7.2 61.9 %copy-start = (bf16[4096,256]{1,0:T(8,128)(2,1)S(1)}, bf16[4096,256]{1,0:T(8,128)(2,1)}, u32[]{:S(2)}) copy-start(bf16[4096,256]{1,0:T(8,128)(2,1)} %param.10) | copy-start | bytes 6291460
  7.2 2.9 %copy-start.6 = (bf16[1,512,256]{2,1,0:T(8,128)(2,1)S(1)}, bf16[1,512,256]{2,1,0:T(8,128)(2,1)}, u32[]{:S(2)}) copy-start(bf16[1,512,256]{2,1,0:T(8,128)(2,1)} %param.8) | copy-start | bytes 786436
  7.2 3.0 %copy-start.7 = (s32[2,8,4]{1,2,0:T(4,128)S(1)}, s32[2,8,4]{1,2,0:T(4,128)}, u32[]{:S(2)}) copy-start(s32[2,8,4]{1,2,0:T(4,128)} %param.9) | copy-start | bytes 772
  7.2 61.9 %all-gather.3.cloned.1.call-start = ((), (), s32[]{:S(2)}) async-start(), calls=%async_computation.2 | async-start | bytes 6291456 | tf_op jit(solution)/shard_map/all_gather | solution.py:55
  9.9 11.6 %copy-start.2 = (bf16[2,256,2,128]{3,2,1,0:T(2,128)(2,1)}, bf16[2,256,2,128]{3,2,1,0:T(2,128)(2,1)S(1)}, u32[]{:S(2)}) copy-start(bf16[2,256,2,128]{3,2,1,0:T(2,128)(2,1)S(1)} %select_n.40) | copy-start | bytes 786436
  10.1 11.2 %copy-start.3 = (bf16[2,256,2,128]{1,3,2,0:T(8,128)(2,1)}, bf16[2,256,2,128]{1,3,2,0:T(8,128)(2,1)S(1)}, u32[]{:S(2)}) copy-start(bf16[2,256,2,128]{1,3,2,0:T(8,128)(2,1)S(1)} %copy.86) | copy-start | bytes 786436
  13.0 32.1 %all-to-all-start = ((f32[4,2,2,128,128]{4,1,3,2,0:T(2,128)}), f32[4,2,2,128,128]{4,1,3,2,0:T(2,128)}, u32[]{:S(2)}, u32[]{:S(2)}) async-start(f32[4,2,2,128,128]{4,1,3,2,0:T(2,128)} %copy.90), calls=%async_computation | async-start | bytes 2097152 | tf_op jit(solution)/shard_map/all_to_all | solution.py:43
  19.3 91.7 %all-gather.5.cloned.1.call-start = ((), (), s32[]{:S(2)}) async-start(), calls=%async_computation.3 | async-start | bytes 1310720 | tf_op jit(solution)/shard_map/all_gather | solution.py:65
  21.5 0.7 copy-start.4
  81.8 65.8 %reduce-scatter.2.cloned.1.call-start = ((), (), s32[]{:S(2)}) async-start(), calls=%async_computation.4 | async-start | bytes 2359296 | tf_op jit(solution)/shard_map/reduce_scatter | solution.py:84
  100.2 0.8 copy-start.1
  108.9 9.2 %copy-start.5 = (f32[2,256,2,128]{1,3,2,0:T(8,128)S(1)}, f32[2,256,2,128]{1,3,2,0:T(8,128)}, u32[]{:S(2)}) copy-start(f32[2,256,2,128]{1,3,2,0:T(8,128)} %copy.113) | copy-start | bytes 1572868
Sparse Core Ops, SparseCore 0:
  9.6 59.4 all-gather.2
  81.9 27.9 all-gather.4
  112.2 35.3 reduce-scatter.1
where the time goes:
time: 157 us; the launch traced here: 156 us
  waiting for transfers between devices  71.8 us (46%)
  matrix products  28.3 us (18%)
  local copies, waits for them, and re-layouts  27.8 us (18%)
  between operations  14 us (9%)
  other arithmetic  7.58 us (5%)
  starting transfers between devices  6.58 us (4%)
    reduce_scatter x1, waiting for transfers between devices, per_device(): lax.psum_scatter(lax.dot_general(grad_rows, attn_flat, (((0,), (0,)), (()...  27.1 us
    all_gather x1, waiting for transfers between devices, per_device(): gathered = lax.all_gather(out_grad, 'head', axis=2, tiled=True)  22.2 us
    all_to_all x1, waiting for transfers between devices, per_device(): lax.all_to_all(presum, 'seq', split_axis=0, concat_axis=0, tiled=True)  21.7 us
    select_n x4, local copies, waits for them, and re-layouts, feature_slope(): return jnp.where(inputs > 0, 1.0, jnp.exp(jnp.minimum(inputs, 0.0)))  8.28 us
    all_to_all x1, starting transfers between devices, per_device(): lax.all_to_all(presum, 'seq', split_axis=0, concat_axis=0, tiled=True)  6.32 us
    dot_general x1, matrix products, per_device(): lax.dot_general(grad_rows, attn_flat, (((0,), (0,)), ((), ())), preferred...  4.88 us
    dot_general x1, matrix products, per_device(): jnp.dot(grad_rows, out_weight, preferred_element_type=f32).astype(bf16)  4.23 us
    reshape x2, local copies, waits for them, and re-layouts, per_device(): grad_f = d_attn.astype(f32).reshape(block_count, BLK, heads_here, DH)  4.13 us
  transfers between devices with their start and end apart: 4, of which 3 were waited for; matrix products, arithmetic and copies ran while one was open for 31% of the time, Pallas kernels for 0%

commit v1 on v0

--- a/solution.py
+++ b/solution.py
@@ -6,6 +6,28 @@
 DH = 128
 BLK = 256
 epsilon = 1e-06
+
+
+def joined_along(blocks, dim):
+    shape = list(blocks.shape[1:])
+    shape[dim] *= blocks.shape[0]
+    return jnp.moveaxis(blocks, 0, dim).reshape(shape)
+
+
+def doubled(x, axis):
+    size = lax.axis_size(axis)
+    parts = x[None]
+    for level in range(size.bit_length() - 1):
+        distance = 1 << level
+        other = lax.ppermute(parts, axis, [(i, i ^ distance) for i in range(size)])
+        both = jnp.stack([parts, other])
+        upper = lax.axis_index(axis) >> level & 1
+        parts = jnp.where(upper == 0, both, both[::-1]).reshape(-1, *x.shape)
+    return parts
+
+
+def collect(value, axis, dim):
+    return joined_along(doubled(value, axis), dim)
 
 
 def feature_map(inputs):
@@ -52,7 +74,7 @@
     rinv = lax.rsqrt(jnp.mean(numer * numer, axis=-1, keepdims=True) + epsilon)
     attn_out = (numer * rinv).astype(bf16)
     attn_flat = attn_out.reshape(tokens_here, heads_here * DH)
-    gathered = lax.all_gather(out_grad, "head", axis=2, tiled=True)
+    gathered = collect(out_grad, "head", 2)
     grad_rows = gathered[0]
     d_attn = jnp.dot(grad_rows, out_weight, preferred_element_type=f32).astype(bf16)
     grad_f = d_attn.astype(f32).reshape(block_count, BLK, heads_here, DH)

time: 157 us -> 141 us (0.90)
  waiting for transfers between devices: 71.8 us -> 50.6 us
  matrix products: 28.3 us -> 24.3 us
  other arithmetic: 7.58 us -> 10.8 us
  local copies, waits for them, and re-layouts: 27.8 us -> 31 us
  between operations: 14 us -> 15.7 us
    all_gather x1 -> x0, waiting for transfers between devices: 22.2 us -> none  [per_device(): gathered = lax.all_gather(out_grad, 'head', axis=2, tiled=True)]
    reduce_scatter x1, waiting for transfers between devices: 27.1 us -> 11.5 us  [per_device(): lax.psum_scatter(lax.dot_general(grad_rows, attn_flat, (((0,), (0,)), (()...]
    ppermute x0 -> x1, waiting for transfers between devices: none -> 9.71 us  [doubled(): other = lax.ppermute(parts, axis, [(i, i ^ distance) for i in range(size)])]
    all_gather x1, waiting for transfers between devices: 0.01 us -> 6.96 us  [per_device(): lax.all_gather(c_grad, 'seq', axis=0, tiled=True)]
    unnamed x17 -> x25, local copies, waits for them, and re-layouts: 3.06 us -> 7.22 us
    ppermute x0 -> x1, starting transfers between devices: none -> 2.94 us  [doubled(): other = lax.ppermute(parts, axis, [(i, i ^ distance) for i in range(size)])]
    another operation x0 -> x1, other arithmetic: none -> 2.61 us  [doubled(): both = jnp.stack([parts, other])]
    dot_general x1, matrix products: 4.23 us -> 2.08 us  [per_device(): jnp.dot(grad_rows, out_weight, preferred_element_type=f32).astype(bf16)]
  transfers between devices with their start and end apart: 4 -> 4, of which waited for: 3 -> 4; matrix products, arithmetic and copies ran while one was open for 31% -> 31% of each run, Pallas kernels for 0% -> 0%
where the time goes in v1:
time: 141 us; the launch traced here: 140 us
  waiting for transfers between devices  50.6 us (36%)
  local copies, waits for them, and re-layouts  31 us (22%)
  matrix products  24.3 us (17%)
  between operations  15.7 us (11%)
  other arithmetic  10.8 us (8%)
  starting transfers between devices  8.03 us (6%)
    all_to_all x1, waiting for transfers between devices, per_device(): lax.all_to_all(presum, 'seq', split_axis=0, concat_axis=0, tiled=True)  22.4 us
    reduce_scatter x1, waiting for transfers between devices, per_device(): lax.psum_scatter(lax.dot_general(grad_rows, attn_flat, (((0,), (0,)), (()...  11.5 us
    ppermute x1, waiting for transfers between devices, doubled(): other = lax.ppermute(parts, axis, [(i, i ^ distance) for i in range(size)])  9.71 us
    select_n x4, local copies, waits for them, and re-layouts, feature_slope(): return jnp.where(inputs > 0, 1.0, jnp.exp(jnp.minimum(inputs, 0.0)))  8.25 us
    unnamed x25, local copies, waits for them, and re-layouts  7.22 us
    all_gather x1, waiting for transfers between devices, per_device(): lax.all_gather(c_grad, 'seq', axis=0, tiled=True)  6.96 us
    all_to_all x1, starting transfers between devices, per_device(): lax.all_to_all(presum, 'seq', split_axis=0, concat_axis=0, tiled=True)  4.87 us
    dot_general x1, matrix products, per_device(): lax.dot_general(grad_rows, attn_flat, (((0,), (0,)), ((), ())), preferred...  4.79 us
  transfers between devices with their start and end apart: 4, of which 4 were waited for; matrix products, arithmetic and copies ran while one was open for 31% of the time, Pallas kernels for 0%

profile of v1, /device:TPU:0, one launch (start us, length us, event | category | flops | bytes accessed | tf_op | source)
XLA Modules:
  0.0 140.4 jit_solution(64807545460536058)
XLA Ops:
  8.0 4.1 %copy.99 = bf16[1,512,2048]{1,2,0:T(8,128)(2,1)} copy(bf16[1,512,2048]{2,1,0:T(8,128)(2,1)} %param.11) | data formatting | bytes 4194304 | tf_op args[5]
  12.1 2.9 %collective-permute-start = (bf16[1,1,512,2048]{2,3,1,0:T(8,128)(2,1)}, bf16[1,1,512,2048]{2,3,1,0:T(8,128)(2,1)}, u32[]{:S(2)}, u32[]{:S(2)}) collective-permute-start(bf16[1,1,512,2048]{2,3,1,0:T(8,128)(2,1)} %bitcast.66), channel_id=1, source_target_pairs={{0,2},{2,0},{1,3},{3,1},{4,6},{6,4},{5,7},{7,5},{8,10},{10,8},{9,1... | collective-permute-start | bytes 6291464 | tf_op jit(solution)/shard_map/ppermute | solution.py:22
  15.1 0.9 fusion.17
  16.4 0.2 fusion.32
  16.6 1.1 fusion.24
  17.8 1.4 copy.91
  19.1 4.9 %all-to-all-start = ((f32[4,2,2,128,128]{4,1,3,2,0:T(2,128)}), f32[4,2,2,128,128]{4,1,3,2,0:T(2,128)}, u32[]{:S(2)}, u32[]{:S(2)}) async-start(f32[4,2,2,128,128]{4,1,3,2,0:T(2,128)} %copy.91), calls=%async_computation | async-start | bytes 2097152 | tf_op jit(solution)/shard_map/all_to_all | solution.py:65
  24.0 1.0 fusion.21
  25.3 0.3 fusion
  25.6 0.4 copy-done.6
  26.0 1.1 convolution_bitcast_fusion
  27.1 22.4 %all-to-all-done = f32[4,2,2,128,128]{4,1,3,2,0:T(2,128)} async-done(((f32[4,2,2,128,128]{4,1,3,2,0:T(2,128)}), f32[4,2,2,128,128]{4,1,3,2,0:T(2,128)}, u32[]{:S(2)}, u32[]{:S(2)}) %all-to-all-start) | async-done | bytes 1048608 | tf_op jit(solution)/shard_map/all_to_all | solution.py:65
  49.6 1.7 %reduce_sum.37 = bf16[2,2,128,128]{3,0,2,1:T(2,128)(2,1)S(1)} reduce(f32[4,2,2,128,128]{4,1,3,2,0:T(2,128)} %all-to-all-done, f32[]{:T(128)} %constant.11.clone.1), dimensions={0}, to_apply=%region_1.2 | reduce | flops 196608 | bytes 1179652 | tf_op jit(solution)/shard_map/reduce_sum | solution.py:66
  51.3 9.7 %collective-permute-done = bf16[1,1,512,2048]{2,3,1,0:T(8,128)(2,1)} collective-permute-done((bf16[1,1,512,2048]{2,3,1,0:T(8,128)(2,1)}, bf16[1,1,512,2048]{2,3,1,0:T(8,128)(2,1)}, u32[]{:S(2)}, u32[]{:S(2)}) %collective-permute-start) | collective-permute-done | bytes 2097184 | tf_op jit(solution)/shard_map/ppermute | solution.py:22
  61.0 2.6 %pad_maximum_fusion = bf16[2,1,1,512,2048]{3,4,0,2,1:T(8,128)(2,1)S(1)} fusion(bf16[1,1,1,512,2048]{3,4,0,2,1:T(8,128)(2,1)} %bitcast.8, bf16[1,1,1,512,2048]{3,4,0,2,1:T(8,128)(2,1)} %bitcast.67), kind=kLoop, calls=%fused_computation.2 | loop fusion | flops 2097152 | bytes 8388608 | tf_op jit(solution)/shard_map/stack | solution.py:23
  63.6 0.8 reverse_select_fusion
  64.4 1.9 %copy-done.2 = bf16[2,1,1,512,2048]{3,4,0,2,1:T(8,128)(2,1)} copy-done((bf16[2,1,1,512,2048]{3,4,0,2,1:T(8,128)(2,1)}, bf16[2,1,1,512,2048]{3,4,0,2,1:T(8,128)(2,1)S(1)}, u32[]{:S(2)}) %copy-start.2) | copy-done | bytes 4194328
  66.3 2.1 %fusion.9 = f32[512,256]{1,0:T(8,128)} fusion(bf16[512,4096]{0,1:T(8,128)(2,1)S(1)} %bitcast.68, bf16[4096,256]{1,0:T(8,128)(2,1)S(1)} %copy-done), kind=kOutput, calls=%fused_computation.20 | convolution fusion | flops 1074003968 | bytes 6815744 | tf_op jit(solution)/shard_map/dot_general | solution.py:79
  68.4 2.1 %reshape.98 = f32[2,256,2,128]{3,2,1,0:T(2,128)} reshape(f32[512,256]{1,0:T(8,128)} %fusion.9) | data formatting | bytes 1048576 | tf_op jit(solution)/shard_map/reshape | solution.py:80
  70.5 2.0 %copy.101 = f32[2,256,2,128]{1,3,2,0:T(8,128)} copy(f32[2,256,2,128]{3,2,1,0:T(2,128)} %reshape.98) | data formatting | bytes 1048576 | tf_op jit(solution)/shard_map/reshape | solution.py:80
  72.6 1.5 %multiply_reduce_fusion = (f32[2,256,2]{1,2,0:T(2,128)S(1)}, f32[2,256,2]{1,2,0:T(2,128)S(1)}, f32[2,256,2,128]{1,3,2,0:T(8,128)S(1)}) fusion(f32[2,256,2,128]{1,3,2,0:T(8,128)} %copy.101, f32[2,256,2,128]{1,3,2,0:T(8,128)} %convolution_bitcast_fusion, bf16[2,256,2,128]{1,3,2,0:T(8,128)(2,1)S(1)} %copy.110, bf16[2,2,128,128]{3,0,2,1:T(2,128)(2,1)S(1)} %reduce_sum.37), kind=kOutput, calls=%fused_computation.41 | convolution fusion | flops 34207744 | bytes 1974272 | tf_op jit(solution)/shard_map/nthd,nhde->nthe/dot_general | solution.py:72
  74.1 1.9 %subtract_convert_fusion = (bf16[2,256,2,128]{1,3,2,0:T(8,128)(2,1)S(1)}, bf16[2,256,2,128]{1,3,2,0:T(8,128)(2,1)}) fusion(f32[2,256,2,128]{1,3,2,0:T(8,128)S(1)} %get-tuple-element.15, f32[2,256,2,128]{1,3,2,0:T(8,128)} %copy.101, f32[2,256,2]{1,2,0:T(2,128)S(1)} %get-tuple-element.16, f32[2,256,2]{1,2,0:T(2,128)S(1)} %get-tuple-element.13, ...), kind=kLoop, calls=%fused_computation.40 | loop fusion | flops 917504 | bytes 1585152 | tf_op jit(solution)/shard_map/convert_element_type | solution.py:82
  76.0 1.0 fusion.43
  77.0 0.2 reduce-scatter.2.cloned.1.call-start
  77.2 1.8 %copy.98 = bf16[2,256,2,128]{3,2,1,0:T(2,128)(2,1)} copy(bf16[2,256,2,128]{1,3,2,0:T(8,128)(2,1)} %get-tuple-element.8) | data formatting | bytes 524288 | tf_op jit(solution)/shard_map/convert_element_type | solution.py:75
  79.0 4.8 %convolution_convert_fusion = bf16[4096,256]{1,0:T(8,128)(2,1)} fusion(bf16[512,4096]{0,1:T(8,128)(2,1)} %bitcast.69, bf16[64,8,2,128]{3,2,1,0:T(2,128)(2,1)} %bitcast.71), kind=kOutput, calls=%fused_computation.1 | convolution fusion | flops 1074790400 | bytes 6553600 | tf_op jit(solution)/shard_map/dot_general | solution.py:107
  83.8 2.1 %select_n.56 = f32[2,256,2,128]{3,2,1,0:T(2,128)} reshape(f32[1,512,256]{2,1,0:T(8,128)} %get-tuple-element.11) | data formatting | bytes 1048576 | tf_op jit(solution)/shard_map/jit(_where)/select_n | solution.py:38
  85.9 2.0 %copy.108 = f32[2,256,2,128]{1,3,2,0:T(8,128)} copy(f32[2,256,2,128]{3,2,1,0:T(2,128)} %select_n.56) | data formatting | bytes 1048576 | tf_op jit(solution)/shard_map/jit(_where)/select_n | solution.py:38
  88.0 2.1 %select_n.58 = f32[2,256,2,128]{3,2,1,0:T(2,128)} reshape(f32[1,512,256]{2,1,0:T(8,128)} %get-tuple-element.9) | data formatting | bytes 1048576 | tf_op jit(solution)/shard_map/jit(_where)/select_n | solution.py:38
  90.0 2.0 %copy.116 = f32[2,256,2,128]{1,3,2,0:T(8,128)} copy(f32[2,256,2,128]{3,2,1,0:T(2,128)} %select_n.58) | data formatting | bytes 1048576 | tf_op jit(solution)/shard_map/jit(_where)/select_n | solution.py:38
  92.1 1.8 %reshape_reshape.3 = bf16[1,512,256]{2,1,0:T(8,128)(2,1)} reshape(bf16[2,256,2,128]{3,2,1,0:T(2,128)(2,1)} %copy.98) | data formatting | bytes 524288 | tf_op jit(solution)/shard_map/reshape;reshape | solution.py:114
  93.9 1.3 fusion.1
  95.2 0.8 copy-done.1
  96.0 1.2 fusion.42
  97.3 2.0 %fusion.7 = bf16[2,256,2,128]{1,3,2,0:T(8,128)(2,1)} fusion(f32[2,256,2,128]{1,3,2,0:T(8,128)} %copy.108, f32[2,2,128,256]{3,2,1,0:T(8,128)S(1)} %fusion.42, bf16[2,256,2,128]{1,3,2,0:T(8,128)(2,1)S(1)} %get-tuple-element.7, bf16[2,2,128,128]{3,0,2,1:T(2,128)(2,1)S(1)} %reduce_sum.37), kind=kOutput, calls=%fused_computation.17 | convolution fusion | flops 33947648 | bytes 1703936 | tf_op jit(solution)/shard_map/nthe,nhde->nthd/dot_general | solution.py:94
  99.2 1.8 %copy.109 = bf16[2,256,2,128]{3,2,1,0:T(2,128)(2,1)} copy(bf16[2,256,2,128]{1,3,2,0:T(8,128)(2,1)} %fusion.7) | data formatting | bytes 524288 | tf_op jit(solution)/shard_map/convert_element_type | solution.py:103
  101.0 1.8 %reshape.93 = bf16[1,512,256]{2,1,0:T(8,128)(2,1)} reshape(bf16[2,256,2,128]{3,2,1,0:T(2,128)(2,1)} %copy.109) | data formatting | bytes 524288 | tf_op jit(solution)/shard_map/reshape | solution.py:103
  102.9 2.1 %fusion.44 = f32[2,2,128,256]{3,2,1,0:T(8,128)} fusion(bf16[2,256,2,128]{1,3,2,0:T(8,128)(2,1)S(1)} %copy.110, bf16[2,2,256,256]{3,2,1,0:T(8,128)(2,1)} %copy-done.1), kind=kOutput, calls=%fused_computation.72 | convolution fusion | flops 67108864 | bytes 1310720 | tf_op jit(solution)/shard_map/nhts,nthd->nshd/dot_general | solution.py:97
  104.9 1.0 fusion.45
  106.0 7.0 %all-gather.2.cloned.1.call-done = f32[8,2,128,128]{3,2,1,0:T(8,128)} async-done(((f32[2,2,128,128]{3,2,1,0:T(8,128)}), f32[8,2,128,128]{3,2,1,0:T(8,128)}) %all-gather.2.cloned.1.call-update) | async-done | bytes 1048592 | tf_op jit(solution)/shard_map/all_gather | solution.py:87
  112.9 2.9 %fusion.12 = bf16[2,2,128,128]{3,0,2,1:T(2,128)(2,1)S(1)} fusion(f32[8,2,128,128]{3,2,1,0:T(8,128)} %all-gather.2.cloned.1.call-done, f32[2,8,8]{2,1,0:T(8,128)S(1)} %convert_reduce_fusion, s32[]{:T(128)S(6)} %select_n.49), kind=kOutput, calls=%fused_computation.24 | convolution fusion | flops 6356992 | bytes 1180164 | tf_op jit(solution)/shard_map/hmk,mhde->khde/dot_general | solution.py:84
  115.9 1.5 %fusion.8 = bf16[2,256,2,128]{1,3,2,0:T(8,128)(2,1)S(1)} fusion(f32[2,256,2,128]{1,3,2,0:T(8,128)} %copy.116, f32[2,2,128,256]{3,2,1,0:T(8,128)} %fusion.44, bf16[2,2,128,128]{2,3,1,0:T(8,128)(2,1)S(1)} %copy.118, bf16[2,256,2,128]{3,2,1,0:T(2,128)(2,1)S(1)} %reshape_squeeze.3), kind=kOutput, calls=%fused_computation.18 | convolution fusion | flops 33947648 | bytes 1703936 | tf_op jit(solution)/shard_map/nshe,nhde->nshd/dot_general | solution.py:96
  117.4 0.2 copy.117
  117.6 0.9 reshape.94
  118.5 0.2 fusion.11
  118.9 0.9 reshape.95
  119.8 11.5 %reduce-scatter.2.cloned.1.call-done = bf16[512,256]{1,0:T(8,128)(2,1)} async-done(((bf16[4096,256]{1,0:T(8,128)(2,1)}), bf16[512,256]{1,0:T(8,128)(2,1)}) %reduce-scatter.2.cloned.1.call-update) | async-done | bytes 262160 | tf_op jit(solution)/shard_map/reduce_scatter | solution.py:106
  131.2 1.8 %convert_element_type.74 = f32[512,256]{1,0:T(8,128)} convert(bf16[512,256]{1,0:T(8,128)(2,1)} %reduce-scatter.2.cloned.1.call-done) | non-fusion elementwise | flops 131072 | bytes 786432 | tf_op jit(solution)/shard_map/convert_element_type | solution.py:113
  (34 shorter events, 1.0 us)
Async XLA Ops:
  8.0 58.3 %copy-start = (bf16[4096,256]{1,0:T(8,128)(2,1)S(1)}, bf16[4096,256]{1,0:T(8,128)(2,1)}, u32[]{:S(2)}) copy-start(bf16[4096,256]{1,0:T(8,128)(2,1)} %param.10) | copy-start | bytes 6291460
  8.0 7.0 %copy-start.9 = (bf16[1,512,256]{2,1,0:T(8,128)(2,1)S(1)}, bf16[1,512,256]{2,1,0:T(8,128)(2,1)}, u32[]{:S(2)}) copy-start(bf16[1,512,256]{2,1,0:T(8,128)(2,1)} %param.7) | copy-start | bytes 786436
  8.0 8.0 %copy-start.11 = (s32[2,8,4]{1,2,0:T(4,128)S(1)}, s32[2,8,4]{1,2,0:T(4,128)}, u32[]{:S(2)}) copy-start(s32[2,8,4]{1,2,0:T(4,128)} %param.9) | copy-start | bytes 772
  8.0 8.1 %copy-start.8 = (bf16[1,512,256]{2,1,0:T(8,128)(2,1)S(1)}, bf16[1,512,256]{2,1,0:T(8,128)(2,1)}, u32[]{:S(2)}) copy-start(bf16[1,512,256]{2,1,0:T(8,128)(2,1)} %param.8) | copy-start | bytes 786436
  12.1 48.9 %collective-permute-start = (bf16[1,1,512,2048]{2,3,1,0:T(8,128)(2,1)}, bf16[1,1,512,2048]{2,3,1,0:T(8,128)(2,1)}, u32[]{:S(2)}, u32[]{:S(2)}) collective-permute-start(bf16[1,1,512,2048]{2,3,1,0:T(8,128)(2,1)} %bitcast.66), channel_id=1, source_target_pairs={{0,2},{2,0},{1,3},{3,1},{4,6},{6,4},{5,7},{7,5},{8,10},{10,8},{9,1... | collective-permute-start | bytes 6291464 | tf_op jit(solution)/shard_map/ppermute | solution.py:22
  16.0 8.0 %copy-start.10 = (bf16[1,512,256]{2,1,0:T(8,128)(2,1)S(1)}, bf16[1,512,256]{2,1,0:T(8,128)(2,1)}, u32[]{:S(2)}) copy-start(bf16[1,512,256]{2,1,0:T(8,128)(2,1)} %param.6) | copy-start | bytes 786436
  16.2 9.1 %copy-start.3 = (bf16[2,256,2,128]{3,2,1,0:T(2,128)(2,1)}, bf16[2,256,2,128]{3,2,1,0:T(2,128)(2,1)S(1)}, u32[]{:S(2)}) copy-start(bf16[2,256,2,128]{3,2,1,0:T(2,128)(2,1)S(1)} %select_n.48) | copy-start | bytes 786436
  16.4 8.6 %copy-start.5 = (bf16[2,256,2,128]{1,3,2,0:T(8,128)(2,1)}, bf16[2,256,2,128]{1,3,2,0:T(8,128)(2,1)S(1)}, u32[]{:S(2)}) copy-start(bf16[2,256,2,128]{1,3,2,0:T(8,128)(2,1)S(1)} %copy.87) | copy-start | bytes 786436
  19.1 30.4 %all-to-all-start = ((f32[4,2,2,128,128]{4,1,3,2,0:T(2,128)}), f32[4,2,2,128,128]{4,1,3,2,0:T(2,128)}, u32[]{:S(2)}, u32[]{:S(2)}) async-start(f32[4,2,2,128,128]{4,1,3,2,0:T(2,128)} %copy.91), calls=%async_computation | async-start | bytes 2097152 | tf_op jit(solution)/shard_map/all_to_all | solution.py:65
  24.0 88.9 %all-gather.2.cloned.1.call-start = ((), (), s32[]{:S(2)}) async-start(), calls=%async_computation.2 | async-start | bytes 1310720 | tf_op jit(solution)/shard_map/all_gather | solution.py:87
  25.3 0.7 copy-start.6
  64.4 2.0 %copy-start.2 = (bf16[2,1,1,512,2048]{3,4,0,2,1:T(8,128)(2,1)}, bf16[2,1,1,512,2048]{3,4,0,2,1:T(8,128)(2,1)S(1)}, u32[]{:S(2)}) copy-start(bf16[2,1,1,512,2048]{3,4,0,2,1:T(8,128)(2,1)S(1)} %reverse_select_fusion) | copy-start | bytes 12582916
  77.0 54.3 %reduce-scatter.2.cloned.1.call-start = ((), (), s32[]{:S(2)}) async-start(), calls=%async_computation.3 | async-start | bytes 2359296 | tf_op jit(solution)/shard_map/reduce_scatter | solution.py:106
  95.2 0.8 copy-start.1
  104.9 13.6 %copy-start.4 = (bf16[2,256,2,128]{3,2,1,0:T(2,128)(2,1)S(1)}, bf16[2,256,2,128]{3,2,1,0:T(2,128)(2,1)}, u32[]{:S(2)}) copy-start(bf16[2,256,2,128]{3,2,1,0:T(2,128)(2,1)} %copy-done.3) | copy-start | bytes 786436
  106.0 12.5 %copy-start.7 = (f32[2,2,128,256]{3,2,1,0:T(8,128)S(1)}, f32[2,2,128,256]{3,2,1,0:T(8,128)}, u32[]{:S(2)}) copy-start(f32[2,2,128,256]{3,2,1,0:T(8,128)} %fusion.45) | copy-start | bytes 1572868
Sparse Core Ops, SparseCore 0:
  77.1 35.7 all-gather.1
Sparse Core Ops, SparseCore 1:
  83.9 47.3 reduce-scatter.1
